TPU v7x, 32 devices: a whole 2x2x4 slice. The times are simulated.
32 devices in a mesh: row: 4 (over y, x), sa: 4 (over z), ha: 2 (over core).
Axes of the slice: x: 2, y: 2, z: 4, core: 2. Of those that a mesh axis runs over, the one named last changes fastest.
Arguments:
- records: float32 [64, 16, 8192], P(None, 'sa', ('row', 'ha')), parts along dimension 2, may hold values from -6 to 6
- halo_mass: float32 [16, 8192], P('sa', ('row', 'ha')), parts along dimension 1, may hold values from 0.1 to 10
- forest_id: int32 [16, 8192], P('sa', ('row', 'ha')), parts along dimension 1, may hold values from 0 to 1023, as said below
- dest_block: int32 [16, 8192], P('sa', ('row', 'ha')), parts along dimension 1, may hold values from 0 to 319, as said below
- dest_slot: int32 [16, 8192], P('sa', ('row', 'ha')), parts along dimension 1, may hold values from 0 to 127
Outputs:
- blocks: float32 [64, 1280, 128], P(None, ('row', 'sa', 'ha')), parts along dimension 1
- block_mass: float32 [1280, 128], P(('row', 'sa', 'ha')), parts along dimension 0
- forest_mass: float32 [4096], P(('row', 'sa', 'ha')), parts along dimension 0
- forest_mean: float32 [64, 4096], P(None, ('row', 'sa', 'ha')), parts along dimension 1
- forest_second: float32 [64, 4096], P(None, ('row', 'sa', 'ha')), parts along dimension 1
There are 4 independent parts, one for each index of `row`. A program takes and returns all parts, laid end to end along the dimension named above; each array names one. Nothing has to cross between parts.
Inputs may be any that keep to these rules, and one draw needn't show every extreme that they name: The pairs (dest_block, dest_slot) are distinct over all halos. Block b lies on the device of index b // 40 of sa+ha (sa slowest), and forest f is owned by the device of index f // 128; every halo goes to a block of its forest's owner. On each device the used slots are the first ones in block-then-slot order, and every forest has at least one halo. `forest_id`: of the halos of one device (one index of sa and one of ha), at most 704 go to blocks of one device; in every draw some pair of devices reaches 704, and some device has all its 5120 slots used.
All inputs are finite; a program needn't handle non-finite values.
Results may differ from a plain program's by a relative error of at most 0.0003.
Values sent between devices are 32-bit elements; how exact they have to be, the bound alone decides.
A program may use at most 64 MiB of HBM per device.

v0:
```python
import jax
import jax.numpy as jnp
from jax import lax
from jax.sharding import PartitionSpec as P

FOR_DEV = 128
BLK_DEV = 40


def tiled_place(source, target, width, tile_cols):
    tile_count = (width + tile_cols - 1) // tile_cols

    def one_tile(tile_index):
        columns = tile_index * tile_cols + jnp.arange(tile_cols, dtype=jnp.int32)
        select = (target[:, None] == columns[None, :]).astype(jnp.float32)
        return jnp.dot(
            source, select, precision=lax.Precision.HIGHEST, preferred_element_type=jnp.float32
        )

    pieces = lax.map(one_tile, jnp.arange(tile_count, dtype=jnp.int32))
    placed = jnp.moveaxis(pieces, 0, 1).reshape(source.shape[0], tile_count * tile_cols)
    return placed


def bucket_ranks(owner_dev, peer_count):
    local_count = owner_dev.shape[0]
    span = 512
    group_count = local_count // span
    member = (
        owner_dev.reshape(group_count, span)[:, :, None]
        == jnp.arange(peer_count, dtype=jnp.int32)[None, None, :]
    ).astype(jnp.bfloat16)
    lower = (jnp.arange(span)[:, None] > jnp.arange(span)[None, :]).astype(jnp.bfloat16)
    within = jnp.einsum("ij,bjp->bip", lower, member, preferred_element_type=jnp.float32)
    totals = jnp.sum(member.astype(jnp.float32), axis=1)
    earlier = (jnp.arange(group_count)[:, None] > jnp.arange(group_count)[None, :]).astype(
        jnp.float32
    )
    before = jnp.dot(
        earlier, totals, precision=lax.Precision.HIGHEST, preferred_element_type=jnp.float32
    )
    counted = (within + before[:, None, :]) * member.astype(jnp.float32)
    return jnp.sum(counted, axis=2).reshape(local_count).astype(jnp.int32)


def on_device(records, halo_mass, forest_id, dest_block, dest_slot):
    sa_count = lax.axis_size("sa")
    ha_count = lax.axis_size("ha")
    peer_count = sa_count * ha_count
    fields = records.shape[0]
    local_count = records.shape[1] * records.shape[2]
    capacity = 11 * (local_count // peer_count) // 8
    slots_dev = BLK_DEV * 128
    width_out = peer_count * capacity
    flat = records.reshape(fields, local_count)
    weights_in = halo_mass.reshape(local_count)
    block_in = dest_block.reshape(local_count)
    forest_in = forest_id.reshape(local_count)
    owner_dev = block_in // BLK_DEV
    target = owner_dev * capacity + bucket_ranks(owner_dev, peer_count)
    slot_local = block_in % BLK_DEV * 128 + dest_slot.reshape(local_count)
    source = jnp.concatenate(
        [
            flat,
            weights_in[None, :],
            (slot_local + 1).astype(jnp.float32)[None, :],
            (forest_in % FOR_DEV + 1).astype(jnp.float32)[None, :],
        ]
    )
    packed = tiled_place(source, target, width_out, min(512, width_out))
    outbox = packed[:fields]
    labels = packed[fields:]
    arrived = (
        lax.all_to_all(
            outbox.reshape(fields, peer_count, capacity),
            ("sa", "ha"),
            split_axis=1,
            concat_axis=1,
            tiled=True,
        ),
        lax.all_to_all(
            labels.reshape(3, peer_count, capacity),
            ("sa", "ha"),
            split_axis=1,
            concat_axis=1,
            tiled=True,
        ),
    )
    incoming = arrived[0].reshape(fields, width_out)
    tags = arrived[1].reshape(3, width_out)
    slot_tag = tags[1].astype(jnp.int32) - 1
    arranged = tiled_place(
        jnp.concatenate([incoming, tags[0:1], tags[2:3]]), slot_tag, slots_dev, 512
    )
    blocks = arranged[:fields]
    slot_mass = arranged[fields]
    slot_forest = arranged[fields + 1].astype(jnp.int32) - 1
    member = (slot_forest[None, :] == jnp.arange(FOR_DEV, dtype=jnp.int32)[:, None]).astype(
        jnp.float32
    )
    scaled = slot_mass[None, :] * blocks
    weighted = jnp.concatenate([slot_mass[None, :], scaled, scaled * blocks])
    owned = lax.dot_general(
        weighted,
        member,
        (((1,), (1,)), ((), ())),
        precision=lax.Precision.HIGHEST,
        preferred_element_type=jnp.float32,
    )
    mass_sum = lax.psum(jnp.sum(weights_in), ("sa", "ha"))
    weight = owned[0]
    forest_mass = weight * (FOR_DEV * peer_count / mass_sum)
    forest_mean = owned[1 : 1 + fields] / weight[None, :]
    forest_second = owned[1 + fields :] / weight[None, :]
    return (
        blocks.reshape(fields, BLK_DEV, 128),
        slot_mass.reshape(BLK_DEV, 128),
        forest_mass,
        forest_mean,
        forest_second,
    )


def solution(mesh):
    in_specs = (
        P(None, "sa", ("row", "ha")),
        P("sa", ("row", "ha")),
        P("sa", ("row", "ha")),
        P("sa", ("row", "ha")),
        P("sa", ("row", "ha")),
    )
    out_specs = (
        P(None, ("row", "sa", "ha"), None),
        P(("row", "sa", "ha"), None),
        P(("row", "sa", "ha")),
        P(None, ("row", "sa", "ha")),
        P(None, ("row", "sa", "ha")),
    )
    return jax.shard_map(
        on_device, mesh=mesh, in_specs=in_specs, out_specs=out_specs, check_vma=False
    )
```

profile of v0, /device:TPU:9, one launch (start us, length us, event | category | flops | bytes accessed | tf_op | source)
XLA Modules:
  0.0 187.3 jit_solution(281483939733563413)
XLA Ops:
  7.8 47.6 %while.20 = (s32[]{:T(128)}, f32[11,67,512]{2,1,0:T(8,128)S(1)}, s32[4096]{0:T(1024)S(1)}, s32[11]{0:T(128)S(1)}, f32[67,4096]{1,0:T(8,128)S(1)}, /*index=5*/s32[]{:T(128)}, s32[1]{0:T(128)}) while((s32[]{:T(128)}, f32[11,67,512]{2,1,0:T(8,128)S(1)}, s32[4096]{0:T(1024)S(1)}, s32[11]{0:T(128)S(1)}, f32[67,4096]{1,0:T(8,128)S(1)}, ...), condition=%wide.region_3.4_spmd, body=%wide.region_2.3_spmd.sunk | while | flops 1688207872 | bytes 1347701 | solution.py:20
  9.0 3.1 %fusion.60 = f32[11,67,512]{2,1,0:T(8,128)S(1)} fusion(f32[11,67,512]{2,1,0:T(8,128)S(1)} %get-tuple-element.163, s32[]{:T(128)S(6)} %copy.43, f32[67,4096]{1,0:T(8,128)S(1)} %get-tuple-element.173, s32[512]{0:T(512)S(1)} %iota_add_fusion.4, s32[4096]{0:T(1024)S(1)} %get-tuple-element.171), kind=kOutput, calls=%fused_computation.5.clone.1 | convolution fusion | flops 1688207360 | bytes 1345540 | tf_op jit(solution)/shard_map/while/body/eval_jaxpr/dot_general | solution.py:16
  17.7 3.1 %fusion.60 = f32[11,67,512]{2,1,0:T(8,128)S(1)} fusion(f32[11,67,512]{2,1,0:T(8,128)S(1)} %get-tuple-element.163, s32[]{:T(128)S(6)} %copy.43, f32[67,4096]{1,0:T(8,128)S(1)} %get-tuple-element.173, s32[512]{0:T(512)S(1)} %iota_add_fusion.4, s32[4096]{0:T(1024)S(1)} %get-tuple-element.171), kind=kOutput, calls=%fused_computation.5.clone.1 | convolution fusion | flops 1688207360 | bytes 1345540 | tf_op jit(solution)/shard_map/while/body/eval_jaxpr/dot_general | solution.py:16
  22.0 3.1 %fusion.60 = f32[11,67,512]{2,1,0:T(8,128)S(1)} fusion(f32[11,67,512]{2,1,0:T(8,128)S(1)} %get-tuple-element.163, s32[]{:T(128)S(6)} %copy.43, f32[67,4096]{1,0:T(8,128)S(1)} %get-tuple-element.173, s32[512]{0:T(512)S(1)} %iota_add_fusion.4, s32[4096]{0:T(1024)S(1)} %get-tuple-element.171), kind=kOutput, calls=%fused_computation.5.clone.1 | convolution fusion | flops 1688207360 | bytes 1345540 | tf_op jit(solution)/shard_map/while/body/eval_jaxpr/dot_general | solution.py:16
  26.3 3.1 %fusion.60 = f32[11,67,512]{2,1,0:T(8,128)S(1)} fusion(f32[11,67,512]{2,1,0:T(8,128)S(1)} %get-tuple-element.163, s32[]{:T(128)S(6)} %copy.43, f32[67,4096]{1,0:T(8,128)S(1)} %get-tuple-element.173, s32[512]{0:T(512)S(1)} %iota_add_fusion.4, s32[4096]{0:T(1024)S(1)} %get-tuple-element.171), kind=kOutput, calls=%fused_computation.5.clone.1 | convolution fusion | flops 1688207360 | bytes 1345540 | tf_op jit(solution)/shard_map/while/body/eval_jaxpr/dot_general | solution.py:16
  30.7 3.1 %fusion.60 = f32[11,67,512]{2,1,0:T(8,128)S(1)} fusion(f32[11,67,512]{2,1,0:T(8,128)S(1)} %get-tuple-element.163, s32[]{:T(128)S(6)} %copy.43, f32[67,4096]{1,0:T(8,128)S(1)} %get-tuple-element.173, s32[512]{0:T(512)S(1)} %iota_add_fusion.4, s32[4096]{0:T(1024)S(1)} %get-tuple-element.171), kind=kOutput, calls=%fused_computation.5.clone.1 | convolution fusion | flops 1688207360 | bytes 1345540 | tf_op jit(solution)/shard_map/while/body/eval_jaxpr/dot_general | solution.py:16
  39.3 3.1 %fusion.60 = f32[11,67,512]{2,1,0:T(8,128)S(1)} fusion(f32[11,67,512]{2,1,0:T(8,128)S(1)} %get-tuple-element.163, s32[]{:T(128)S(6)} %copy.43, f32[67,4096]{1,0:T(8,128)S(1)} %get-tuple-element.173, s32[512]{0:T(512)S(1)} %iota_add_fusion.4, s32[4096]{0:T(1024)S(1)} %get-tuple-element.171), kind=kOutput, calls=%fused_computation.5.clone.1 | convolution fusion | flops 1688207360 | bytes 1345540 | tf_op jit(solution)/shard_map/while/body/eval_jaxpr/dot_general | solution.py:16
  48.0 3.1 %fusion.60 = f32[11,67,512]{2,1,0:T(8,128)S(1)} fusion(f32[11,67,512]{2,1,0:T(8,128)S(1)} %get-tuple-element.163, s32[]{:T(128)S(6)} %copy.43, f32[67,4096]{1,0:T(8,128)S(1)} %get-tuple-element.173, s32[512]{0:T(512)S(1)} %iota_add_fusion.4, s32[4096]{0:T(1024)S(1)} %get-tuple-element.171), kind=kOutput, calls=%fused_computation.5.clone.1 | convolution fusion | flops 1688207360 | bytes 1345540 | tf_op jit(solution)/shard_map/while/body/eval_jaxpr/dot_general | solution.py:16
  52.3 3.1 %fusion.60 = f32[11,67,512]{2,1,0:T(8,128)S(1)} fusion(f32[11,67,512]{2,1,0:T(8,128)S(1)} %get-tuple-element.163, s32[]{:T(128)S(6)} %copy.43, f32[67,4096]{1,0:T(8,128)S(1)} %get-tuple-element.173, s32[512]{0:T(512)S(1)} %iota_add_fusion.4, s32[4096]{0:T(1024)S(1)} %get-tuple-element.171), kind=kOutput, calls=%fused_computation.5.clone.1 | convolution fusion | flops 1688207360 | bytes 1345540 | tf_op jit(solution)/shard_map/while/body/eval_jaxpr/dot_general | solution.py:16
  56.2 5.6 %all-to-all-start = ((f32[3,8,704]{2,0,1:T(4,128)}), f32[3,8,704]{2,0,1:T(4,128)S(1)}, u32[]{:S(2)}, u32[]{:S(2)}) async-start(f32[3,8,704]{2,0,1:T(4,128)} %copy.22), calls=%async_computation | async-start | bytes 196608 | tf_op jit(solution)/shard_map/all_to_all | solution.py:81
  64.8 3.1 %copy.24 = f32[64,8,704]{2,0,1:T(8,128)} copy(f32[64,8,704]{2,1,0:T(8,128)} %reshape.226) | data formatting | bytes 2883584 | tf_op jit(solution)/shard_map/reshape | solution.py:75
  67.9 5.2 %all-to-all-start.1 = ((f32[64,8,704]{2,0,1:T(8,128)}), f32[64,8,704]{2,0,1:T(8,128)S(1)}, u32[]{:S(2)}, u32[]{:S(2)}) async-start(f32[64,8,704]{2,0,1:T(8,128)} %copy.24), calls=%async_computation.1 | async-start | bytes 3145728 | tf_op jit(solution)/shard_map/all_to_all | solution.py:74
  73.7 41.3 %psum.7 = f32[]{:T(128)} all-reduce(f32[]{:T(128)} %reduce_sum.29), channel_id=1, replica_groups=mesh['row'=4,'sa'=4,'ha'=2] {'sa','ha'}, use_global_device_ids=true, to_apply=%region_7.8 | all-reduce | flops 1 | bytes 8 | tf_op jit(solution)/shard_map/psum | solution.py:110
  117.9 60.4 %while.21 = (s32[]{:T(128)}, f32[10,66,512]{2,1,0:T(8,128)}, s32[5632]{0:T(1024)S(1)}, s32[10]{0:T(128)S(1)}, f32[66,5632]{1,0:T(8,128)S(1)}, /*index=5*/s32[]{:T(128)}, s32[1]{0:T(128)}) while((s32[]{:T(128)}, f32[10,66,512]{2,1,0:T(8,128)}, s32[5632]{0:T(1024)S(1)}, s32[10]{0:T(128)S(1)}, f32[66,5632]{1,0:T(8,128)S(1)}, ...), condition=%wide.region_5.6_spmd, body=%wide.region_4.5_spmd.sunk | while | flops 2286682624 | bytes 1661045 | solution.py:20
  119.1 4.8 %fusion.63 = f32[10,66,512]{2,1,0:T(8,128)} fusion(f32[10,66,512]{2,1,0:T(8,128)} %get-tuple-element.184, s32[]{:T(128)S(6)} %copy.49, f32[66,5632]{1,0:T(8,128)S(1)} %get-tuple-element.194, s32[512]{0:T(512)S(1)} %iota_add_fusion.5, s32[5632]{0:T(1024)S(1)} %get-tuple-element.192), kind=kOutput, calls=%fused_computation.12.clone.1 | convolution fusion | flops 2286682112 | bytes 1658884 | tf_op jit(solution)/shard_map/while/body/eval_jaxpr/dot_general | solution.py:16
  125.2 4.8 %fusion.63 = f32[10,66,512]{2,1,0:T(8,128)} fusion(f32[10,66,512]{2,1,0:T(8,128)} %get-tuple-element.184, s32[]{:T(128)S(6)} %copy.49, f32[66,5632]{1,0:T(8,128)S(1)} %get-tuple-element.194, s32[512]{0:T(512)S(1)} %iota_add_fusion.5, s32[5632]{0:T(1024)S(1)} %get-tuple-element.192), kind=kOutput, calls=%fused_computation.12.clone.1 | convolution fusion | flops 2286682112 | bytes 1658884 | tf_op jit(solution)/shard_map/while/body/eval_jaxpr/dot_general | solution.py:16
  131.2 4.8 %fusion.63 = f32[10,66,512]{2,1,0:T(8,128)} fusion(f32[10,66,512]{2,1,0:T(8,128)} %get-tuple-element.184, s32[]{:T(128)S(6)} %copy.49, f32[66,5632]{1,0:T(8,128)S(1)} %get-tuple-element.194, s32[512]{0:T(512)S(1)} %iota_add_fusion.5, s32[5632]{0:T(1024)S(1)} %get-tuple-element.192), kind=kOutput, calls=%fused_computation.12.clone.1 | convolution fusion | flops 2286682112 | bytes 1658884 | tf_op jit(solution)/shard_map/while/body/eval_jaxpr/dot_general | solution.py:16
  137.3 4.8 %fusion.63 = f32[10,66,512]{2,1,0:T(8,128)} fusion(f32[10,66,512]{2,1,0:T(8,128)} %get-tuple-element.184, s32[]{:T(128)S(6)} %copy.49, f32[66,5632]{1,0:T(8,128)S(1)} %get-tuple-element.194, s32[512]{0:T(512)S(1)} %iota_add_fusion.5, s32[5632]{0:T(1024)S(1)} %get-tuple-element.192), kind=kOutput, calls=%fused_computation.12.clone.1 | convolution fusion | flops 2286682112 | bytes 1658884 | tf_op jit(solution)/shard_map/while/body/eval_jaxpr/dot_general | solution.py:16
  143.3 4.8 %fusion.63 = f32[10,66,512]{2,1,0:T(8,128)} fusion(f32[10,66,512]{2,1,0:T(8,128)} %get-tuple-element.184, s32[]{:T(128)S(6)} %copy.49, f32[66,5632]{1,0:T(8,128)S(1)} %get-tuple-element.194, s32[512]{0:T(512)S(1)} %iota_add_fusion.5, s32[5632]{0:T(1024)S(1)} %get-tuple-element.192), kind=kOutput, calls=%fused_computation.12.clone.1 | convolution fusion | flops 2286682112 | bytes 1658884 | tf_op jit(solution)/shard_map/while/body/eval_jaxpr/dot_general | solution.py:16
  149.3 4.8 %fusion.63 = f32[10,66,512]{2,1,0:T(8,128)} fusion(f32[10,66,512]{2,1,0:T(8,128)} %get-tuple-element.184, s32[]{:T(128)S(6)} %copy.49, f32[66,5632]{1,0:T(8,128)S(1)} %get-tuple-element.194, s32[512]{0:T(512)S(1)} %iota_add_fusion.5, s32[5632]{0:T(1024)S(1)} %get-tuple-element.192), kind=kOutput, calls=%fused_computation.12.clone.1 | convolution fusion | flops 2286682112 | bytes 1658884 | tf_op jit(solution)/shard_map/while/body/eval_jaxpr/dot_general | solution.py:16
  155.4 4.8 %fusion.63 = f32[10,66,512]{2,1,0:T(8,128)} fusion(f32[10,66,512]{2,1,0:T(8,128)} %get-tuple-element.184, s32[]{:T(128)S(6)} %copy.49, f32[66,5632]{1,0:T(8,128)S(1)} %get-tuple-element.194, s32[512]{0:T(512)S(1)} %iota_add_fusion.5, s32[5632]{0:T(1024)S(1)} %get-tuple-element.192), kind=kOutput, calls=%fused_computation.12.clone.1 | convolution fusion | flops 2286682112 | bytes 1658884 | tf_op jit(solution)/shard_map/while/body/eval_jaxpr/dot_general | solution.py:16
  161.4 4.8 %fusion.63 = f32[10,66,512]{2,1,0:T(8,128)} fusion(f32[10,66,512]{2,1,0:T(8,128)} %get-tuple-element.184, s32[]{:T(128)S(6)} %copy.49, f32[66,5632]{1,0:T(8,128)S(1)} %get-tuple-element.194, s32[512]{0:T(512)S(1)} %iota_add_fusion.5, s32[5632]{0:T(1024)S(1)} %get-tuple-element.192), kind=kOutput, calls=%fused_computation.12.clone.1 | convolution fusion | flops 2286682112 | bytes 1658884 | tf_op jit(solution)/shard_map/while/body/eval_jaxpr/dot_general | solution.py:16
  167.5 4.8 %fusion.63 = f32[10,66,512]{2,1,0:T(8,128)} fusion(f32[10,66,512]{2,1,0:T(8,128)} %get-tuple-element.184, s32[]{:T(128)S(6)} %copy.49, f32[66,5632]{1,0:T(8,128)S(1)} %get-tuple-element.194, s32[512]{0:T(512)S(1)} %iota_add_fusion.5, s32[5632]{0:T(1024)S(1)} %get-tuple-element.192), kind=kOutput, calls=%fused_computation.12.clone.1 | convolution fusion | flops 2286682112 | bytes 1658884 | tf_op jit(solution)/shard_map/while/body/eval_jaxpr/dot_general | solution.py:16
  173.5 4.8 %fusion.63 = f32[10,66,512]{2,1,0:T(8,128)} fusion(f32[10,66,512]{2,1,0:T(8,128)} %get-tuple-element.184, s32[]{:T(128)S(6)} %copy.49, f32[66,5632]{1,0:T(8,128)S(1)} %get-tuple-element.194, s32[512]{0:T(512)S(1)} %iota_add_fusion.5, s32[5632]{0:T(1024)S(1)} %get-tuple-element.192), kind=kOutput, calls=%fused_computation.12.clone.1 | convolution fusion | flops 2286682112 | bytes 1658884 | tf_op jit(solution)/shard_map/while/body/eval_jaxpr/dot_general | solution.py:16
  (101 shorter events, 44.0 us)
Async XLA Ops:
  56.2 11.7 %all-to-all-start = ((f32[3,8,704]{2,0,1:T(4,128)}), f32[3,8,704]{2,0,1:T(4,128)S(1)}, u32[]{:S(2)}, u32[]{:S(2)}) async-start(f32[3,8,704]{2,0,1:T(4,128)} %copy.22), calls=%async_computation | async-start | bytes 196608 | tf_op jit(solution)/shard_map/all_to_all | solution.py:81
  67.9 5.2 %copy-start.1 = (f32[4,1024]{1,0:T(4,128)S(1)}, f32[4,1024]{1,0:T(4,128)}, u32[]{:S(2)}) copy-start(f32[4,1024]{1,0:T(4,128)} %param.10) | copy-start | bytes 49156
  67.9 48.3 %all-to-all-start.1 = ((f32[64,8,704]{2,0,1:T(8,128)}), f32[64,8,704]{2,0,1:T(8,128)S(1)}, u32[]{:S(2)}, u32[]{:S(2)}) async-start(f32[64,8,704]{2,0,1:T(8,128)} %copy.24), calls=%async_computation.1 | async-start | bytes 3145728 | tf_op jit(solution)/shard_map/all_to_all | solution.py:74
  179.2 2.9 %copy-start = (f32[1,10,512]{2,0,1:T(1,128)}, f32[1,10,512]{2,0,1:T(1,128)S(1)}, u32[]{:S(2)}) copy-start(f32[1,10,512]{2,0,1:T(1,128)S(1)} %slice.70) | copy-start | bytes 61444
where the time goes:
time: 189 us; the launch traced here: 187 us
  matrix products  84 us (44%)
  blocking collectives  41.3 us (22%)
  local copies, waits for them, and re-layouts  29.8 us (16%)
  loops' own time  14 us (7%)
  starting transfers between devices  10.8 us (6%)
  other arithmetic  5.79 us (3%)
    dot_general x21, matrix products, one_tile(): jnp.dot(source, select, precision=lax.Precision.HIGHEST, preferred_elemen...  81.6 us
    psum x1, blocking collectives, on_device(): mass_sum = lax.psum(jnp.sum(weights_in), ('sa', 'ha'))  41.3 us
    another operation x2, loops' own time, tiled_place(): pieces = lax.map(one_tile, jnp.arange(tile_count, dtype=jnp.int32))  14 us
    dynamic_slice x21, local copies, waits for them, and re-layouts, tiled_place(): pieces = lax.map(one_tile, jnp.arange(tile_count, dtype=jnp.int32))  12.3 us
    all_to_all x1, starting transfers between devices, on_device(): lax.all_to_all(labels.reshape(3, peer_count, capacity), ('sa', 'ha'), spl...  5.6 us
    unnamed x11, local copies, waits for them, and re-layouts  5.57 us
    all_to_all x1, starting transfers between devices, on_device(): lax.all_to_all(outbox.reshape(fields, peer_count, capacity), ('sa', 'ha')...  5.23 us
    reshape x2, local copies, waits for them, and re-layouts, on_device(): outbox.reshape(fields, peer_count, capacity)  5.1 us
  transfers between devices with their start and end apart: 2, of which 0 were waited for; matrix products, arithmetic and copies ran while one was open for 4% of the time, Pallas kernels for 0%

commit v1 on v0

v1 whole, which is shorter than its diff:
```python
import functools

import jax
import jax.numpy as jnp
from jax import lax
from jax.experimental import pallas as pl
from jax.experimental.pallas import tpu as pltpu
from jax.sharding import PartitionSpec as P

FOR_DEV = 128
BLK_DEV = 40
LANES = 128
LABELS = 4


def round_up(value, unit):
    return (value + unit - 1) // unit * unit


class Plan:
    def __init__(self, fields, snaps, halos, peers):
        self.fields, self.snaps, self.halos, self.peers = fields, snaps, halos, peers
        self.local = snaps * halos
        self.tiles = self.local // LANES
        self.chunks = halos // LANES
        capacity = 11 * (self.local // peers) // 8
        self.cap = round_up(capacity, 16)
        self.half = self.cap // 2
        self.groups = LANES // LABELS
        self.lab_rows = round_up((self.cap + self.groups - 1) // self.groups, 8)
        self.rows = self.half + self.lab_rows
        self.slots = BLK_DEV * LANES
        self.per_tile = LANES // self.lab_rows
        self.lab_tiles = (peers + self.per_tile - 1) // self.per_tile
        assert 2 * fields == LANES


def pack_kernel(plan, rec_ref, mass_ref, forest_ref, block_ref, slot_ref, out_ref,
                rows_in, rows_out, flat, members, target, target_s, sem):
    snaps, fields, peers, tiles = plan.snaps, plan.fields, plan.peers, plan.tiles
    for chunk in range(plan.chunks):
        here = pl.ds(chunk * snaps, snaps)
        cut = pl.ds(chunk * LANES, LANES)
        flat[0, here, :] = block_ref[:, cut].astype(jnp.float32)
        flat[1, here, :] = slot_ref[:, cut].astype(jnp.float32)
        flat[2, here, :] = forest_ref[:, cut].astype(jnp.float32)
        flat[3, here, :] = mass_ref[:, cut]
    block = flat[0]
    mass = flat[3]
    for owner in range(peers):
        inside = (block >= owner * BLK_DEV) & (block < (owner + 1) * BLK_DEV)
        members[pl.ds(owner * tiles, tiles), :] = jnp.where(inside, 1.0, 0.0).astype(jnp.bfloat16)
    down = lax.broadcasted_iota(jnp.int32, (LANES, LANES), 0)
    across = lax.broadcasted_iota(jnp.int32, (LANES, LANES), 1)
    upper = jnp.where(down < across, 1.0, 0.0).astype(jnp.bfloat16)
    every = jnp.ones((LANES, LANES), jnp.bfloat16)
    lower = jnp.where(
        lax.broadcasted_iota(jnp.int32, (tiles, tiles), 0)
        > lax.broadcasted_iota(jnp.int32, (tiles, tiles), 1), 1.0, 0.0).astype(jnp.bfloat16)
    place = jnp.zeros((tiles, LANES), jnp.float32)
    owner_of = jnp.zeros((tiles, LANES), jnp.float32)
    for owner in range(peers):
        member = members[pl.ds(owner * tiles, tiles), :]
        within = jnp.dot(member, upper, preferred_element_type=jnp.float32)
        totals = jnp.dot(member, every, preferred_element_type=jnp.float32).astype(jnp.bfloat16)
        before = jnp.dot(lower, totals, preferred_element_type=jnp.float32)
        chosen = member.astype(jnp.float32)
        place = place + chosen * (within + before + float(owner * plan.cap))
        owner_of = owner_of + chosen * float(owner)
    target[...] = place.astype(jnp.int32)
    copy = pltpu.make_async_copy(target, target_s, sem)
    copy.start()
    flat[1] = (block - owner_of * float(BLK_DEV)) * float(LANES) + flat[1]
    flat[2] = flat[2] - owner_of * float(FOR_DEV)
    total = jnp.sum(mass)

    sub = lax.broadcasted_iota(jnp.int32, (8, LANES), 0)
    zeros = jnp.zeros((LANES - fields - 8, LANES), jnp.float32)
    for chunk in range(plan.chunks):
        for snap in range(snaps):
            row = chunk * snaps + snap
            values = rec_ref[:, snap, pl.ds(chunk * LANES, LANES)]
            label = jnp.where(sub == 0, flat[3, pl.ds(row, 1), :], total)
            label = jnp.where(sub == 1, flat[1, pl.ds(row, 1), :], label)
            label = jnp.where(sub == 2, flat[2, pl.ds(row, 1), :], label)
            whole = jnp.concatenate([values, label, zeros], axis=0)
            rows_in[pl.ds(row * LANES, LANES), :] = whole.T

    lane = lax.broadcasted_iota(jnp.int32, (8, LANES), 1)
    empty = jnp.where(lane == fields + 1, float(plan.slots),
                      jnp.where(lane == fields + 3, total, 0.0))

    def clear(step, carry):
        for part in range(8):
            rows_out[pl.ds(pl.multiple_of(step * 64 + part * 8, 8), 8), :] = empty
        return carry

    lax.fori_loop(0, peers * plan.cap // 64, clear, 0)
    copy.wait()

    def scatter(row, carry):
        for col in range(LANES):
            to = target_s[row, col]
            rows_out[pl.ds(to, 1), :] = rows_in[pl.ds(row * LANES + col, 1), :]
        return carry

    lax.fori_loop(0, tiles, scatter, 0)

    def squeeze(peer, carry):
        start = peer * plan.cap
        for step in range(plan.half // 8):
            low = rows_out[pl.ds(pl.multiple_of(start + step * 8, 8), 8), :]
            high = rows_out[pl.ds(pl.multiple_of(start + plan.half + step * 8, 8), 8), :]
            out_ref[peer, pl.ds(step * 8, 8), :] = jnp.where(
                lane < fields, low, pltpu.roll(high, fields, 1))
        per = plan.lab_rows // 8
        for part in range(per):
            gathered = jnp.zeros((8, LANES), jnp.float32)
            for group in range(plan.groups):
                tile = group * per + part
                if tile * 8 < plan.cap:
                    piece = rows_out[pl.ds(pl.multiple_of(start + tile * 8, 8), 8), :]
                    moved = pltpu.roll(piece, (group * LABELS - fields) % LANES, 1)
                    gathered = jnp.where(lane // LABELS == group, moved, gathered)
            out_ref[peer, pl.ds(plan.half + part * 8, 8), :] = gathered
        return carry

    lax.fori_loop(0, peers, squeeze, 0)


def exchange_kernel(plan, n_ha, send_ref, recv_ref, send_sem, recv_sem, own_sem):
    peers = plan.peers
    me = lax.axis_index("sa") * n_ha + lax.axis_index("ha")
    barrier = pltpu.get_barrier_semaphore()

    def where_is(peer):
        return {"sa": peer // n_ha, "ha": lax.rem(peer, n_ha)}

    for step in range(1, peers):
        pl.semaphore_signal(barrier, inc=1, device_id=where_is(lax.rem(me + step, peers)),
                            device_id_type=pl.DeviceIdType.MESH)
    pl.semaphore_wait(barrier, peers - 1)
    copies = []
    for step in range(1, peers):
        peer = lax.rem(me + step, peers)
        copy = pltpu.make_async_remote_copy(
            src_ref=send_ref.at[peer],
            dst_ref=recv_ref.at[me],
            send_sem=send_sem.at[step],
            recv_sem=recv_sem.at[step],
            device_id=where_is(peer),
            device_id_type=pl.DeviceIdType.MESH,
        )
        copy.start()
        copies.append(copy)
    own = pltpu.make_async_copy(send_ref.at[me], recv_ref.at[me], own_sem)
    own.start()
    own.wait()
    for copy in copies:
        copy.wait()


def unpack_kernel(plan, got_ref, blocks_ref, mass_ref, fmass_ref, mean_ref, second_ref,
                  arrived, placed, labels, labels_s, sems):
    fields, peers = plan.fields, plan.peers
    per = plan.lab_rows // 8
    lane = lax.broadcasted_iota(jnp.int32, (8, LANES), 1)
    copies = []
    for tile in range(plan.lab_tiles):
        first = tile * plan.per_tile
        count = min(plan.per_tile, peers - first)
        pieces = [got_ref[first + k, pl.ds(plan.half, plan.lab_rows), :] for k in range(count)]
        rest = LANES - count * plan.lab_rows
        if rest:
            pieces.append(jnp.zeros((rest, LANES), jnp.float32))
        labels[tile] = jnp.concatenate(pieces, axis=0).T.astype(jnp.int32)
        copy = pltpu.make_async_copy(labels.at[tile], labels_s.at[tile], sems.at[tile])
        copy.start()
        copies.append(copy)

    def clear(step, carry):
        for part in range(8):
            placed[pl.ds(pl.multiple_of(step * 64 + part * 8, 8), 8), :] = jnp.zeros(
                (8, LANES), jnp.float32)
        return carry

    lax.fori_loop(0, plan.slots // 64, clear, 0)
    in_labels = (lane >= fields) & (lane < fields + LABELS)

    def spread(peer, carry):
        start = peer * plan.cap
        for step in range(plan.half // 8):
            both = got_ref[peer, pl.ds(step * 8, 8), :]
            for side in range(2):
                tile = side * (plan.half // 8) + step
                group, part = tile // per, tile % per
                label = got_ref[peer, pl.ds(plan.half + part * 8, 8), :]
                label = pltpu.roll(label, (fields - group * LABELS) % LANES, 1)
                record = both if side == 0 else pltpu.roll(both, fields, 1)
                arrived[pl.ds(pl.multiple_of(start + tile * 8, 8), 8), :] = jnp.where(
                    lane < fields, record, jnp.where(in_labels, label, 0.0))
        return carry

    lax.fori_loop(0, peers, spread, 0)
    for copy in copies:
        copy.wait()

    for peer in range(peers):
        tile, offset = peer // plan.per_tile, peer % plan.per_tile * plan.lab_rows
        whole = plan.cap // plan.lab_rows

        def scatter(group, carry, rows=plan.lab_rows, peer=peer, tile=tile, offset=offset):
            for row in range(rows):
                to = labels_s[tile, group * LABELS + 1, offset + row]
                placed[pl.ds(to, 1), :] = arrived[
                    pl.ds(peer * plan.cap + group * plan.lab_rows + row, 1), :]
            return carry

        lax.fori_loop(0, whole, scatter, 0)
        if plan.cap % plan.lab_rows:
            scatter(whole, 0, rows=plan.cap % plan.lab_rows)

    total = jnp.zeros((1, 1), jnp.float32)
    for peer in range(peers):
        total = total + arrived[pl.ds(peer * plan.cap, 1), :][:, fields + 3:fields + 4]
    forests = lax.broadcasted_iota(jnp.int32, (FOR_DEV, LANES), 0).astype(jnp.float32)
    wide = lax.broadcasted_iota(jnp.int32, (LANES, LANES), 1)

    def one_block(block, carry):
        sums, weights = carry
        rows = placed[pl.ds(pl.multiple_of(block * LANES, LANES), LANES), :]
        turned = rows.T
        blocks_ref[pl.ds(block, fields, stride=BLK_DEV), :] = turned[:fields]
        mass_row = turned[fields:fields + 1]
        mass_ref[pl.ds(block, 1), :] = mass_row
        hit = turned[fields + 2:fields + 3] == forests
        weights = weights + jnp.where(hit, mass_row, 0.0)
        member = jnp.where(hit, 1.0, 0.0).astype(jnp.bfloat16)
        mass = rows[:, fields:fields + 1]
        value = jnp.where(wide < fields, rows, pltpu.roll(rows, fields, 1))
        scaled = mass * value
        scaled = jnp.where(wide < fields, scaled, scaled * value)
        high = scaled.astype(jnp.bfloat16)
        low = (scaled - high.astype(jnp.float32)).astype(jnp.bfloat16)
        sums = sums + jnp.dot(member, high, preferred_element_type=jnp.float32)
        sums = sums + jnp.dot(member, low, preferred_element_type=jnp.float32)
        return sums, weights

    zero = jnp.zeros((FOR_DEV, LANES), jnp.float32)
    sums, weights = lax.fori_loop(0, BLK_DEV, one_block, (zero, zero))
    weight = jnp.sum(weights.T, axis=0, keepdims=True)
    sums = sums.T
    fmass_ref[...] = weight * (float(FOR_DEV * peers) / total)
    mean_ref[...] = sums[:fields] / weight
    second_ref[...] = sums[fields:] / weight


def on_device(n_ha, peers, records, halo_mass, forest_id, dest_block, dest_slot):
    fields, snaps, halos = records.shape
    plan = Plan(fields, snaps, halos, peers)
    f32, i32 = jnp.float32, jnp.int32
    vmem = pl.BlockSpec(memory_space=pltpu.VMEM)
    big = pltpu.CompilerParams(vmem_limit_bytes=48 * 1024 * 1024)
    send = pl.pallas_call(
        functools.partial(pack_kernel, plan),
        out_shape=jax.ShapeDtypeStruct((peers, plan.rows, LANES), f32),
        in_specs=[vmem] * 5,
        out_specs=vmem,
        scratch_shapes=[
            pltpu.VMEM((plan.local, LANES), f32),
            pltpu.VMEM((peers * plan.cap, LANES), f32),
            pltpu.VMEM((4, plan.tiles, LANES), f32),
            pltpu.VMEM((peers * plan.tiles, LANES), jnp.bfloat16),
            pltpu.VMEM((plan.tiles, LANES), i32),
            pltpu.SMEM((plan.tiles, LANES), i32),
            pltpu.SemaphoreType.DMA,
        ],
        compiler_params=big,
        name="pack",
    )(records, halo_mass, forest_id, dest_block, dest_slot)
    got = pl.pallas_call(
        functools.partial(exchange_kernel, plan, n_ha),
        out_shape=jax.ShapeDtypeStruct(send.shape, f32),
        in_specs=[pl.BlockSpec(memory_space=pl.ANY)],
        out_specs=pl.BlockSpec(memory_space=pl.ANY),
        scratch_shapes=[
            pltpu.SemaphoreType.DMA((peers,)),
            pltpu.SemaphoreType.DMA((peers,)),
            pltpu.SemaphoreType.DMA,
        ],
        compiler_params=pltpu.CompilerParams(collective_id=0, has_side_effects=True),
        name="exchange",
    )(send)
    blocks, block_mass, forest_mass, mean, second = pl.pallas_call(
        functools.partial(unpack_kernel, plan),
        out_shape=(
            jax.ShapeDtypeStruct((fields * BLK_DEV, LANES), f32),
            jax.ShapeDtypeStruct((BLK_DEV, LANES), f32),
            jax.ShapeDtypeStruct((1, FOR_DEV), f32),
            jax.ShapeDtypeStruct((fields, FOR_DEV), f32),
            jax.ShapeDtypeStruct((fields, FOR_DEV), f32),
        ),
        in_specs=[vmem],
        out_specs=(vmem,) * 5,
        scratch_shapes=[
            pltpu.VMEM((peers * plan.cap, LANES), f32),
            pltpu.VMEM((plan.slots + 8, LANES), f32),
            pltpu.VMEM((plan.lab_tiles, LANES, LANES), i32),
            pltpu.SMEM((plan.lab_tiles, LANES, LANES), i32),
            pltpu.SemaphoreType.DMA((plan.lab_tiles,)),
        ],
        compiler_params=big,
        name="unpack",
    )(got)
    return (
        blocks.reshape(fields, BLK_DEV, LANES),
        block_mass,
        forest_mass.reshape(FOR_DEV),
        mean,
        second,
    )


def solution(mesh):
    n_ha = mesh.shape["ha"]
    peers = mesh.shape["sa"] * n_ha
    in_specs = (
        P(None, "sa", ("row", "ha")),
        P("sa", ("row", "ha")),
        P("sa", ("row", "ha")),
        P("sa", ("row", "ha")),
        P("sa", ("row", "ha")),
    )
    out_specs = (
        P(None, ("row", "sa", "ha"), None),
        P(("row", "sa", "ha"), None),
        P(("row", "sa", "ha")),
        P(None, ("row", "sa", "ha")),
        P(None, ("row", "sa", "ha")),
    )
    return jax.shard_map(
        functools.partial(on_device, n_ha, peers),
        mesh=mesh, in_specs=in_specs, out_specs=out_specs, check_vma=False
    )
```

time: 189 us -> 73.1 us (0.39)
  matrix products: 84 us -> 0 us
  Pallas kernels: 0 us -> 65.3 us
  blocking collectives: 41.3 us -> 0 us
  local copies, waits for them, and re-layouts: 29.8 us -> 6.61 us
  loops' own time: 14 us -> 0 us
  starting transfers between devices: 10.8 us -> 0 us
  other arithmetic: 5.79 us -> 0 us
    dot_general x24 -> x0, matrix products: 84 us -> none  [the longest x21 81.6 us: one_tile(): jnp.dot(source, select, precision=lax.Precision.HIGHEST, preferred_elemen...]
    pallas_call x0 -> x3, Pallas kernels: none -> 65.3 us  [the longest x1 37.5 us: on_device(): pl.pallas_call(functools.partial(exchange_kernel, plan, n_ha), out_shape=...]
    psum x1 -> x0, blocking collectives: 41.3 us -> none  [on_device(): mass_sum = lax.psum(jnp.sum(weights_in), ('sa', 'ha'))]
    another operation x2 -> x0, loops' own time: 14 us -> none  [tiled_place(): pieces = lax.map(one_tile, jnp.arange(tile_count, dtype=jnp.int32))]
    dynamic_slice x21 -> x0, local copies, waits for them, and re-layouts: 12.3 us -> none  [tiled_place(): pieces = lax.map(one_tile, jnp.arange(tile_count, dtype=jnp.int32))]
    all_to_all x2 -> x0, starting transfers between devices: 10.8 us -> none  [the longest x1 5.6 us: on_device(): lax.all_to_all(labels.reshape(3, peer_count, capacity), ('sa', 'ha'), spl...]
    reshape x6 -> x0, local copies, waits for them, and re-layouts: 7.69 us -> none  [the longest x2 5.1 us: on_device(): outbox.reshape(fields, peer_count, capacity)]
    slice x10 -> x0, local copies, waits for them, and re-layouts: 3.19 us -> none  [the longest x2 1 us: on_device(): outbox = packed[:fields]]
  transfers between devices with their start and end apart: 2 -> 0, of which waited for: 0 -> 0; matrix products, arithmetic and copies ran while one was open for 4% -> 0% of each run, Pallas kernels for 0% -> 0%
where the time goes in v1:
time: 73.1 us; the launch traced here: 72.6 us
  Pallas kernels  65.3 us (89%)
  local copies, waits for them, and re-layouts  6.61 us (9%)
    pallas_call x1, Pallas kernels, on_device(): pl.pallas_call(functools.partial(exchange_kernel, plan, n_ha), out_shape=...  37.5 us
    pallas_call x1, Pallas kernels, on_device(): pl.pallas_call(functools.partial(unpack_kernel, plan), out_shape=(jax.Sha...  20.5 us
    pallas_call x1, Pallas kernels, on_device(): pl.pallas_call(functools.partial(pack_kernel, plan), out_shape=jax.ShapeD...  7.27 us
    unnamed x14, local copies, waits for them, and re-layouts  6.61 us

profile of v1, /device:TPU:9, one launch (start us, length us, event | category | flops | bytes accessed | tf_op | source)
XLA Modules:
  0.0 72.6 jit_solution(15389446414164429680)
XLA Ops:
  0.6 0.0 copy-start.2
  0.6 1.2 %copy-done.2 = f32[64,4,1024]{2,1,0:T(4,128)S(1)} copy-done((f32[64,4,1024]{2,1,0:T(4,128)S(1)}, f32[64,4,1024]{2,1,0:T(4,128)}, u32[]{:S(2)}) %copy-start.2) | copy-done | bytes 1048600
  1.9 0.0 copy-start.3
  1.9 0.7 copy-done.3
  2.6 0.0 copy-start.4
  2.6 0.7 copy-done.4
  3.3 0.0 copy-start.5
  3.3 0.7 copy-done.5
  4.0 0.0 copy-start.6
  4.0 0.7 copy-done.6
  4.7 7.3 %pack.1.send_ref = f32[8,376,128]{2,1,0:T(8,128)S(1)} custom-call(f32[64,4,1024]{2,1,0:T(4,128)S(1)} %copy-done.2, f32[4,1024]{1,0:T(4,128)S(1)} %copy-done.3, s32[4,1024]{1,0:T(4,128)S(1)} %copy-done.4, s32[4,1024]{1,0:T(4,128)S(1)} %copy-done.5, s32[4,1024]{1,0:T(4,128)S(1)} %copy-done.6), custom_call_target="tpu_custom_call" | custom-call | tf_op jit(solution)/shard_map/pack/pallas_call | solution.py:264
  12.0 0.0 copy-start.1
  12.0 1.1 %copy-done.1 = f32[8,376,128]{2,1,0:T(8,128)} copy-done((f32[8,376,128]{2,1,0:T(8,128)}, f32[8,376,128]{2,1,0:T(8,128)S(1)}, u32[]{:S(2)}) %copy-start.1) | copy-done | bytes 1540120
  13.2 37.5 %exchange.1.got_ref = f32[8,376,128]{2,1,0:T(8,128)} custom-call(f32[8,376,128]{2,1,0:T(8,128)} %copy-done.1), custom_call_target="tpu_custom_call" | custom-call | tf_op jit(solution)/shard_map/exchange/pallas_call | solution.py:281
  50.7 0.0 copy-start
  50.7 1.4 %copy-done = f32[8,376,128]{2,1,0:T(8,128)S(1)} copy-done((f32[8,376,128]{2,1,0:T(8,128)S(1)}, f32[8,376,128]{2,1,0:T(8,128)}, u32[]{:S(2)}) %copy-start) | copy-done | bytes 1540120
  52.1 20.5 %unpack.1 = (f32[2560,128]{1,0:T(8,128)}, f32[40,128]{1,0:T(8,128)}, f32[1,128]{1,0:T(1,128)}, f32[64,128]{1,0:T(8,128)}, f32[64,128]{1,0:T(8,128)}) custom-call(f32[8,376,128]{2,1,0:T(8,128)S(1)} %copy-done), custom_call_target="tpu_custom_call" | custom-call | tf_op jit(solution)/shard_map/unpack/pallas_call | solution.py:294
Async XLA Ops:
  0.6 1.2 %copy-start.2 = (f32[64,4,1024]{2,1,0:T(4,128)S(1)}, f32[64,4,1024]{2,1,0:T(4,128)}, u32[]{:S(2)}) copy-start(f32[64,4,1024]{2,1,0:T(4,128)} %rec_ref.1) | copy-start | bytes 3145732
  1.9 0.7 copy-start.3
  2.6 0.7 copy-start.4
  3.3 0.7 copy-start.5
  4.0 0.7 copy-start.6
  12.0 1.1 %copy-start.1 = (f32[8,376,128]{2,1,0:T(8,128)}, f32[8,376,128]{2,1,0:T(8,128)S(1)}, u32[]{:S(2)}) copy-start(f32[8,376,128]{2,1,0:T(8,128)S(1)} %pack.1.send_ref) | copy-start | bytes 4620292
  50.7 1.4 %copy-start = (f32[8,376,128]{2,1,0:T(8,128)S(1)}, f32[8,376,128]{2,1,0:T(8,128)}, u32[]{:S(2)}) copy-start(f32[8,376,128]{2,1,0:T(8,128)} %exchange.1.got_ref) | copy-start | bytes 4620292

commit v2 on v1

--- a/solution.py
+++ b/solution.py
@@ -35,9 +35,21 @@
         assert 2 * fields == LANES
 
 
-def pack_kernel(plan, rec_ref, mass_ref, forest_ref, block_ref, slot_ref, out_ref,
-                rows_in, rows_out, flat, members, target, target_s, sem):
+def pack_kernel(plan, rec_hbm, mass_hbm, forest_hbm, block_hbm, slot_hbm, out_ref,
+                rec_ref, mass_ref, forest_ref, block_ref, slot_ref,
+                rows_in, rows_out, packed, flat, members, target, target_s, sem, in_sems,
+                out_sems):
     snaps, fields, peers, tiles = plan.snaps, plan.fields, plan.peers, plan.tiles
+    loads = []
+    for index, (source, held) in enumerate((
+            (block_hbm, block_ref), (slot_hbm, slot_ref), (forest_hbm, forest_ref),
+            (mass_hbm, mass_ref), (rec_hbm, rec_ref))):
+        load = pltpu.make_async_copy(source, held, in_sems.at[index])
+        load.start()
+        loads.append(load)
+    lane = lax.broadcasted_iota(jnp.int32, (8, LANES), 1)
+    for load in loads[:4]:
+        load.wait()
     for chunk in range(plan.chunks):
         here = pl.ds(chunk * snaps, snaps)
         cut = pl.ds(chunk * LANES, LANES)
@@ -74,6 +86,7 @@
     flat[2] = flat[2] - owner_of * float(FOR_DEV)
     total = jnp.sum(mass)
 
+    loads[4].wait()
     sub = lax.broadcasted_iota(jnp.int32, (8, LANES), 0)
     zeros = jnp.zeros((LANES - fields - 8, LANES), jnp.float32)
     for chunk in range(plan.chunks):
@@ -86,7 +99,6 @@
             whole = jnp.concatenate([values, label, zeros], axis=0)
             rows_in[pl.ds(row * LANES, LANES), :] = whole.T
 
-    lane = lax.broadcasted_iota(jnp.int32, (8, LANES), 1)
     empty = jnp.where(lane == fields + 1, float(plan.slots),
                       jnp.where(lane == fields + 3, total, 0.0))
 
@@ -111,7 +123,7 @@
         for step in range(plan.half // 8):
             low = rows_out[pl.ds(pl.multiple_of(start + step * 8, 8), 8), :]
             high = rows_out[pl.ds(pl.multiple_of(start + plan.half + step * 8, 8), 8), :]
-            out_ref[peer, pl.ds(step * 8, 8), :] = jnp.where(
+            packed[peer, pl.ds(step * 8, 8), :] = jnp.where(
                 lane < fields, low, pltpu.roll(high, fields, 1))
         per = plan.lab_rows // 8
         for part in range(per):
@@ -122,30 +134,45 @@
                     piece = rows_out[pl.ds(pl.multiple_of(start + tile * 8, 8), 8), :]
                     moved = pltpu.roll(piece, (group * LABELS - fields) % LANES, 1)
                     gathered = jnp.where(lane // LABELS == group, moved, gathered)
-            out_ref[peer, pl.ds(plan.half + part * 8, 8), :] = gathered
+            packed[peer, pl.ds(plan.half + part * 8, 8), :] = gathered
+        pltpu.make_async_copy(packed.at[peer], out_ref.at[peer], out_sems.at[peer]).start()
         return carry
 
     lax.fori_loop(0, peers, squeeze, 0)
-
-
-def exchange_kernel(plan, n_ha, send_ref, recv_ref, send_sem, recv_sem, own_sem):
-    peers = plan.peers
+    for peer in range(peers):
+        pltpu.make_async_copy(packed.at[peer], out_ref.at[peer], out_sems.at[peer]).wait()
+
+
+def partner(me, step, peers):
+    if peers & (peers - 1):
+        return lax.rem(me + step, peers)
+    other, bit = jnp.int32(0), 1
+    while bit < peers:
+        mine = lax.rem(lax.div(me, jnp.int32(bit)), jnp.int32(2))
+        other = other + bit * (1 - mine if step & bit else mine)
+        bit *= 2
+    return other
+
+
+def exchange_kernel(plan, n_ha, send_ref, arrived_ref, labels_ref, got_ref,
+                    send_sem, recv_sem, own_sem):
+    fields, peers = plan.fields, plan.peers
     me = lax.axis_index("sa") * n_ha + lax.axis_index("ha")
     barrier = pltpu.get_barrier_semaphore()
 
     def where_is(peer):
-        return {"sa": peer // n_ha, "ha": lax.rem(peer, n_ha)}
-
-    for step in range(1, peers):
-        pl.semaphore_signal(barrier, inc=1, device_id=where_is(lax.rem(me + step, peers)),
+        return {"sa": lax.div(peer, jnp.int32(n_ha)), "ha": lax.rem(peer, jnp.int32(n_ha))}
+
+    others = [partner(me, step, peers) for step in range(1, peers)]
+    for peer in others:
+        pl.semaphore_signal(barrier, inc=1, device_id=where_is(peer),
                             device_id_type=pl.DeviceIdType.MESH)
     pl.semaphore_wait(barrier, peers - 1)
     copies = []
-    for step in range(1, peers):
-        peer = lax.rem(me + step, peers)
+    for step, peer in enumerate(others, 1):
         copy = pltpu.make_async_remote_copy(
             src_ref=send_ref.at[peer],
-            dst_ref=recv_ref.at[me],
+            dst_ref=got_ref.at[step],
             send_sem=send_sem.at[step],
             recv_sem=recv_sem.at[step],
             device_id=where_is(peer),
@@ -153,19 +180,40 @@
         )
         copy.start()
         copies.append(copy)
-    own = pltpu.make_async_copy(send_ref.at[me], recv_ref.at[me], own_sem)
+    own = pltpu.make_async_copy(send_ref.at[me], got_ref.at[0], own_sem)
     own.start()
     own.wait()
-    for copy in copies:
-        copy.wait()
-
-
-def unpack_kernel(plan, got_ref, blocks_ref, mass_ref, fmass_ref, mean_ref, second_ref,
-                  arrived, placed, labels, labels_s, sems):
-    fields, peers = plan.fields, plan.peers
+
     per = plan.lab_rows // 8
     lane = lax.broadcasted_iota(jnp.int32, (8, LANES), 1)
-    copies = []
+    in_labels = (lane >= fields) & (lane < fields + LABELS)
+
+    def spread(step):
+        start = step * plan.cap
+        for tile in range(plan.cap // 8):
+            side, at = tile // (plan.half // 8), tile % (plan.half // 8)
+            record = got_ref[step, pl.ds(at * 8, 8), :]
+            group, part = tile // per, tile % per
+            label = got_ref[step, pl.ds(plan.half + part * 8, 8), :]
+            label = pltpu.roll(label, (fields - group * LABELS) % LANES, 1)
+            if side:
+                record = pltpu.roll(record, fields, 1)
+            arrived_ref[pl.ds(pl.multiple_of(start + tile * 8, 8), 8), :] = jnp.where(
+                lane < fields, record, jnp.where(in_labels, label, 0.0))
+
+    spread(0)
+    peer_of = others[0]
+
+    def arrive(step, carry):
+        pltpu.make_async_remote_copy(
+            src_ref=send_ref.at[0], dst_ref=got_ref.at[step],
+            send_sem=send_sem.at[step], recv_sem=recv_sem.at[step],
+            device_id=where_is(peer_of), device_id_type=pl.DeviceIdType.MESH,
+        ).wait_recv()
+        spread(step)
+        return carry
+
+    lax.fori_loop(1, peers, arrive, 0)
     for tile in range(plan.lab_tiles):
         first = tile * plan.per_tile
         count = min(plan.per_tile, peers - first)
@@ -173,10 +221,16 @@
         rest = LANES - count * plan.lab_rows
         if rest:
             pieces.append(jnp.zeros((rest, LANES), jnp.float32))
-        labels[tile] = jnp.concatenate(pieces, axis=0).T.astype(jnp.int32)
-        copy = pltpu.make_async_copy(labels.at[tile], labels_s.at[tile], sems.at[tile])
-        copy.start()
-        copies.append(copy)
+        labels_ref[tile] = jnp.concatenate(pieces, axis=0).T.astype(jnp.int32)
+    for copy in copies:
+        copy.wait_send()
+
+
+def unpack_kernel(plan, arrived, labels, blocks_ref, mass_ref, fmass_ref, mean_ref,
+                  second_ref, placed, member_s, value_s, labels_s, sem):
+    fields, peers = plan.fields, plan.peers
+    copy = pltpu.make_async_copy(labels, labels_s, sem)
+    copy.start()
 
     def clear(step, carry):
         for part in range(8):
@@ -185,25 +239,7 @@
         return carry
 
     lax.fori_loop(0, plan.slots // 64, clear, 0)
-    in_labels = (lane >= fields) & (lane < fields + LABELS)
-
-    def spread(peer, carry):
-        start = peer * plan.cap
-        for step in range(plan.half // 8):
-            both = got_ref[peer, pl.ds(step * 8, 8), :]
-            for side in range(2):
-                tile = side * (plan.half // 8) + step
-                group, part = tile // per, tile % per
-                label = got_ref[peer, pl.ds(plan.half + part * 8, 8), :]
-                label = pltpu.roll(label, (fields - group * LABELS) % LANES, 1)
-                record = both if side == 0 else pltpu.roll(both, fields, 1)
-                arrived[pl.ds(pl.multiple_of(start + tile * 8, 8), 8), :] = jnp.where(
-                    lane < fields, record, jnp.where(in_labels, label, 0.0))
-        return carry
-
-    lax.fori_loop(0, peers, spread, 0)
-    for copy in copies:
-        copy.wait()
+    copy.wait()
 
     for peer in range(peers):
         tile, offset = peer // plan.per_tile, peer % plan.per_tile * plan.lab_rows
@@ -226,28 +262,37 @@
     forests = lax.broadcasted_iota(jnp.int32, (FOR_DEV, LANES), 0).astype(jnp.float32)
     wide = lax.broadcasted_iota(jnp.int32, (LANES, LANES), 1)
 
-    def one_block(block, carry):
-        sums, weights = carry
-        rows = placed[pl.ds(pl.multiple_of(block * LANES, LANES), LANES), :]
-        turned = rows.T
-        blocks_ref[pl.ds(block, fields, stride=BLK_DEV), :] = turned[:fields]
-        mass_row = turned[fields:fields + 1]
-        mass_ref[pl.ds(block, 1), :] = mass_row
-        hit = turned[fields + 2:fields + 3] == forests
-        weights = weights + jnp.where(hit, mass_row, 0.0)
-        member = jnp.where(hit, 1.0, 0.0).astype(jnp.bfloat16)
-        mass = rows[:, fields:fields + 1]
-        value = jnp.where(wide < fields, rows, pltpu.roll(rows, fields, 1))
-        scaled = mass * value
-        scaled = jnp.where(wide < fields, scaled, scaled * value)
-        high = scaled.astype(jnp.bfloat16)
-        low = (scaled - high.astype(jnp.float32)).astype(jnp.bfloat16)
-        sums = sums + jnp.dot(member, high, preferred_element_type=jnp.float32)
-        sums = sums + jnp.dot(member, low, preferred_element_type=jnp.float32)
-        return sums, weights
-
-    zero = jnp.zeros((FOR_DEV, LANES), jnp.float32)
-    sums, weights = lax.fori_loop(0, BLK_DEV, one_block, (zero, zero))
+    weights = jnp.zeros((FOR_DEV, LANES), jnp.float32)
+    span = 4
+
+    def some_blocks(part, weights):
+        for inner in range(span):
+            block = part * span + inner
+            rows = placed[pl.ds(pl.multiple_of(block * LANES, LANES), LANES), :]
+            turned = rows.T
+            blocks_ref[pl.ds(block, fields, stride=BLK_DEV), :] = turned[:fields]
+            mass_row = turned[fields:fields + 1]
+            mass_ref[pl.ds(block, 1), :] = mass_row
+            hit = turned[fields + 2:fields + 3] == forests
+            weights = weights + jnp.where(hit, mass_row, 0.0)
+            member_s[part, :, inner * LANES:(inner + 1) * LANES] = jnp.where(
+                hit, 1.0, 0.0).astype(jnp.bfloat16)
+            mass = rows[:, fields:fields + 1]
+            value = jnp.where(wide < fields, rows, pltpu.roll(rows, fields, 1))
+            scaled = mass * value
+            scaled = jnp.where(wide < fields, scaled, scaled * value)
+            high = scaled.astype(jnp.bfloat16)
+            low = (scaled - high.astype(jnp.float32)).astype(jnp.bfloat16)
+            here = pl.ds(inner * LANES, LANES)
+            value_s[part, here, :LANES] = high
+            value_s[part, here, LANES:] = low
+        return weights
+
+    weights = lax.fori_loop(0, BLK_DEV // span, some_blocks, weights)
+    sums = jnp.zeros((FOR_DEV, 2 * LANES), jnp.float32)
+    for part in range(BLK_DEV // span):
+        sums = sums + jnp.dot(member_s[part], value_s[part], preferred_element_type=jnp.float32)
+    sums = sums[:, :LANES] + sums[:, LANES:]
     weight = jnp.sum(weights.T, axis=0, keepdims=True)
     sums = sums.T
     fmass_ref[...] = weight * (float(FOR_DEV * peers) / total)
@@ -259,36 +304,52 @@
     fields, snaps, halos = records.shape
     plan = Plan(fields, snaps, halos, peers)
     f32, i32 = jnp.float32, jnp.int32
+    hbm = pl.BlockSpec(memory_space=pltpu.HBM)
     vmem = pl.BlockSpec(memory_space=pltpu.VMEM)
+    full = pltpu.CompilerParams(vmem_limit_bytes=67043328)
     big = pltpu.CompilerParams(vmem_limit_bytes=48 * 1024 * 1024)
     send = pl.pallas_call(
         functools.partial(pack_kernel, plan),
         out_shape=jax.ShapeDtypeStruct((peers, plan.rows, LANES), f32),
-        in_specs=[vmem] * 5,
-        out_specs=vmem,
+        in_specs=[hbm] * 5,
+        out_specs=hbm,
         scratch_shapes=[
+            pltpu.VMEM(records.shape, f32),
+            pltpu.VMEM((snaps, halos), f32),
+            pltpu.VMEM((snaps, halos), i32),
+            pltpu.VMEM((snaps, halos), i32),
+            pltpu.VMEM((snaps, halos), i32),
             pltpu.VMEM((plan.local, LANES), f32),
             pltpu.VMEM((peers * plan.cap, LANES), f32),
+            pltpu.VMEM((peers, plan.rows, LANES), f32),
             pltpu.VMEM((4, plan.tiles, LANES), f32),
             pltpu.VMEM((peers * plan.tiles, LANES), jnp.bfloat16),
             pltpu.VMEM((plan.tiles, LANES), i32),
             pltpu.SMEM((plan.tiles, LANES), i32),
             pltpu.SemaphoreType.DMA,
+            pltpu.SemaphoreType.DMA((5,)),
+            pltpu.SemaphoreType.DMA((peers,)),
         ],
-        compiler_params=big,
+        compiler_params=full,
         name="pack",
     )(records, halo_mass, forest_id, dest_block, dest_slot)
-    got = pl.pallas_call(
+    kept = (peers * plan.cap + plan.lab_tiles * LANES + 1024) * LANES * 4
+    arrived, labels = pl.pallas_call(
         functools.partial(exchange_kernel, plan, n_ha),
-        out_shape=jax.ShapeDtypeStruct(send.shape, f32),
-        in_specs=[pl.BlockSpec(memory_space=pl.ANY)],
-        out_specs=pl.BlockSpec(memory_space=pl.ANY),
+        out_shape=(
+            jax.ShapeDtypeStruct((peers * plan.cap, LANES), f32),
+            jax.ShapeDtypeStruct((plan.lab_tiles, LANES, LANES), i32),
+        ),
+        in_specs=[hbm],
+        out_specs=(vmem, vmem),
         scratch_shapes=[
+            pltpu.VMEM(send.shape, f32),
             pltpu.SemaphoreType.DMA((peers,)),
             pltpu.SemaphoreType.DMA((peers,)),
             pltpu.SemaphoreType.DMA,
         ],
-        compiler_params=pltpu.CompilerParams(collective_id=0, has_side_effects=True),
+        compiler_params=pltpu.CompilerParams(
+            collective_id=0, has_side_effects=True, vmem_limit_bytes=67043328 - kept),
         name="exchange",
     )(send)
     blocks, block_mass, forest_mass, mean, second = pl.pallas_call(
@@ -300,18 +361,18 @@
             jax.ShapeDtypeStruct((fields, FOR_DEV), f32),
             jax.ShapeDtypeStruct((fields, FOR_DEV), f32),
         ),
-        in_specs=[vmem],
+        in_specs=[vmem, vmem],
         out_specs=(vmem,) * 5,
         scratch_shapes=[
-            pltpu.VMEM((peers * plan.cap, LANES), f32),
             pltpu.VMEM((plan.slots + 8, LANES), f32),
-            pltpu.VMEM((plan.lab_tiles, LANES, LANES), i32),
+            pltpu.VMEM((10, FOR_DEV, 4 * LANES), jnp.bfloat16),
+            pltpu.VMEM((10, 4 * LANES, 2 * LANES), jnp.bfloat16),
             pltpu.SMEM((plan.lab_tiles, LANES, LANES), i32),
-            pltpu.SemaphoreType.DMA((plan.lab_tiles,)),
+            pltpu.SemaphoreType.DMA,
         ],
         compiler_params=big,
         name="unpack",
-    )(got)
+    )(arrived, labels)
     return (
         blocks.reshape(fields, BLK_DEV, LANES),
         block_mass,

time: 73.1 us -> 64.5 us (0.88)
  Pallas kernels: 65.3 us -> 60.9 us
  local copies, waits for them, and re-layouts: 6.61 us -> 2.71 us
    pallas_call x1, Pallas kernels: 20.5 us -> 12.7 us  [on_device(): pl.pallas_call(functools.partial(unpack_kernel, plan), out_shape=(jax.Sha...]
    unnamed x14 -> x4, local copies, waits for them, and re-layouts: 6.61 us -> 2.71 us
    pallas_call x1, Pallas kernels: 37.5 us -> 39.5 us  [on_device(): pl.pallas_call(functools.partial(exchange_kernel, plan, n_ha), out_shape=...]
    pallas_call x1, Pallas kernels: 7.27 us -> 8.69 us  [on_device(): pl.pallas_call(functools.partial(pack_kernel, plan), out_shape=jax.ShapeD...]
where the time goes in v2:
time: 64.5 us; the launch traced here: 64.2 us
  Pallas kernels  60.9 us (94%)
  local copies, waits for them, and re-layouts  2.71 us (4%)
  between operations  0.66 us (1%)
    pallas_call x1, Pallas kernels, on_device(): pl.pallas_call(functools.partial(exchange_kernel, plan, n_ha), out_shape=...  39.5 us
    pallas_call x1, Pallas kernels, on_device(): pl.pallas_call(functools.partial(unpack_kernel, plan), out_shape=(jax.Sha...  12.7 us
    pallas_call x1, Pallas kernels, on_device(): pl.pallas_call(functools.partial(pack_kernel, plan), out_shape=jax.ShapeD...  8.69 us
    unnamed x4, local copies, waits for them, and re-layouts  2.71 us

profile of v2, /device:TPU:9, one launch (start us, length us, event | category | flops | bytes accessed | tf_op | source)
XLA Modules:
  0.0 64.2 jit_solution(11907832003930919523)
XLA Ops:
  0.6 8.7 %pack.1.send_ref = f32[8,376,128]{2,1,0:T(8,128)} custom-call(f32[64,4,1024]{2,1,0:T(4,128)} %rec_hbm.1, f32[4,1024]{1,0:T(4,128)} %mass_hbm.1, s32[4,1024]{1,0:T(4,128)} %forest_hbm.1, s32[4,1024]{1,0:T(4,128)} %block_hbm.1, s32[4,1024]{1,0:T(4,128)} %slot_hbm.1), custom_call_target="tpu_custom_call" | custom-call | tf_op jit(solution)/shard_map/pack/pallas_call | solution.py:311
  9.3 39.5 %exchange.1 = (f32[5632,128]{1,0:T(8,128)}, s32[2,128,128]{2,1,0:T(8,128)}) custom-call(f32[8,376,128]{2,1,0:T(8,128)} %pack.1.send_ref), custom_call_target="tpu_custom_call" | custom-call | tf_op jit(solution)/shard_map/exchange/pallas_call | solution.py:337
  48.8 0.0 copy-start
  48.9 1.8 %copy-done = f32[5632,128]{1,0:T(8,128)S(1)} copy-done((f32[5632,128]{1,0:T(8,128)S(1)}, f32[5632,128]{1,0:T(8,128)}, u32[]{:S(2)}) %copy-start) | copy-done | bytes 2883608
  50.7 0.0 copy-start.1
  50.7 0.9 %copy-done.1 = s32[2,128,128]{2,1,0:T(8,128)S(1)} copy-done((s32[2,128,128]{2,1,0:T(8,128)S(1)}, s32[2,128,128]{2,1,0:T(8,128)}, u32[]{:S(2)}) %copy-start.1) | copy-done | bytes 131096
  51.6 12.7 %unpack.1 = (f32[2560,128]{1,0:T(8,128)}, f32[40,128]{1,0:T(8,128)}, f32[1,128]{1,0:T(1,128)}, f32[64,128]{1,0:T(8,128)}, f32[64,128]{1,0:T(8,128)}) custom-call(f32[5632,128]{1,0:T(8,128)S(1)} %copy-done, s32[2,128,128]{2,1,0:T(8,128)S(1)} %copy-done.1), custom_call_target="tpu_custom_call" | custom-call | tf_op jit(solution)/shard_map/unpack/pallas_call | solution.py:355
Async XLA Ops:
  48.8 1.8 %copy-start = (f32[5632,128]{1,0:T(8,128)S(1)}, f32[5632,128]{1,0:T(8,128)}, u32[]{:S(2)}) copy-start(f32[5632,128]{1,0:T(8,128)} %get-tuple-element.12.arrived) | copy-start | bytes 8650756
  50.7 0.9 %copy-start.1 = (s32[2,128,128]{2,1,0:T(8,128)S(1)}, s32[2,128,128]{2,1,0:T(8,128)}, u32[]{:S(2)}) copy-start(s32[2,128,128]{2,1,0:T(8,128)} %get-tuple-element.13.labels) | copy-start | bytes 393220

commit v3 on v2

--- a/solution.py
+++ b/solution.py
@@ -154,8 +154,8 @@
     return other
 
 
-def exchange_kernel(plan, n_ha, send_ref, arrived_ref, labels_ref, got_ref,
-                    send_sem, recv_sem, own_sem):
+def exchange_kernel(plan, n_ha, send_ref, arrived_hbm, labels_hbm, got_ref, arrived_ref,
+                    labels_ref, send_sem, recv_sem, own_sem, out_sems):
     fields, peers = plan.fields, plan.peers
     me = lax.axis_index("sa") * n_ha + lax.axis_index("ha")
     barrier = pltpu.get_barrier_semaphore()
@@ -200,6 +200,12 @@
                 record = pltpu.roll(record, fields, 1)
             arrived_ref[pl.ds(pl.multiple_of(start + tile * 8, 8), 8), :] = jnp.where(
                 lane < fields, record, jnp.where(in_labels, label, 0.0))
+        put(step).start()
+
+    def put(step):
+        here = pl.ds(pl.multiple_of(step * plan.cap, 8), plan.cap)
+        return pltpu.make_async_copy(
+            arrived_ref.at[here, :], arrived_hbm.at[here, :], out_sems.at[step])
 
     spread(0)
     peer_of = others[0]
@@ -222,15 +228,28 @@
         if rest:
             pieces.append(jnp.zeros((rest, LANES), jnp.float32))
         labels_ref[tile] = jnp.concatenate(pieces, axis=0).T.astype(jnp.int32)
+    put_labels = pltpu.make_async_copy(labels_ref, labels_hbm, out_sems.at[peers])
+    put_labels.start()
     for copy in copies:
         copy.wait_send()
-
-
-def unpack_kernel(plan, arrived, labels, blocks_ref, mass_ref, fmass_ref, mean_ref,
-                  second_ref, placed, member_s, value_s, labels_s, sem):
+    for step in range(peers):
+        put(step).wait()
+    put_labels.wait()
+
+
+def unpack_kernel(plan, arrived_hbm, labels, blocks_ref, mass_ref, fmass_ref, mean_ref,
+                  second_ref, arrived, placed, member_s, value_s, labels_s, sem, in_sems):
     fields, peers = plan.fields, plan.peers
+
+    def take(step):
+        here = pl.ds(pl.multiple_of(step * plan.cap, 8), plan.cap)
+        return pltpu.make_async_copy(
+            arrived_hbm.at[here, :], arrived.at[here, :], in_sems.at[step])
+
     copy = pltpu.make_async_copy(labels, labels_s, sem)
     copy.start()
+    for step in range(peers):
+        take(step).start()
 
     def clear(step, carry):
         for part in range(8):
@@ -241,20 +260,18 @@
     lax.fori_loop(0, plan.slots // 64, clear, 0)
     copy.wait()
 
-    for peer in range(peers):
-        tile, offset = peer // plan.per_tile, peer % plan.per_tile * plan.lab_rows
-        whole = plan.cap // plan.lab_rows
-
-        def scatter(group, carry, rows=plan.lab_rows, peer=peer, tile=tile, offset=offset):
-            for row in range(rows):
-                to = labels_s[tile, group * LABELS + 1, offset + row]
-                placed[pl.ds(to, 1), :] = arrived[
-                    pl.ds(peer * plan.cap + group * plan.lab_rows + row, 1), :]
-            return carry
-
-        lax.fori_loop(0, whole, scatter, 0)
-        if plan.cap % plan.lab_rows:
-            scatter(whole, 0, rows=plan.cap % plan.lab_rows)
+    def scatter(peer, carry):
+        tile = lax.div(peer, jnp.int32(plan.per_tile))
+        offset = lax.rem(peer, jnp.int32(plan.per_tile)) * plan.lab_rows
+        start = peer * plan.cap
+        take(peer).wait()
+        for rank in range(plan.cap):
+            group, row = rank // plan.lab_rows, rank % plan.lab_rows
+            to = labels_s[tile, group * LABELS + 1, offset + row]
+            placed[pl.ds(to, 1), :] = arrived[pl.ds(start + rank, 1), :]
+        return carry
+
+    lax.fori_loop(0, peers, scatter, 0)
 
     total = jnp.zeros((1, 1), jnp.float32)
     for peer in range(peers):
@@ -307,7 +324,6 @@
     hbm = pl.BlockSpec(memory_space=pltpu.HBM)
     vmem = pl.BlockSpec(memory_space=pltpu.VMEM)
     full = pltpu.CompilerParams(vmem_limit_bytes=67043328)
-    big = pltpu.CompilerParams(vmem_limit_bytes=48 * 1024 * 1024)
     send = pl.pallas_call(
         functools.partial(pack_kernel, plan),
         out_shape=jax.ShapeDtypeStruct((peers, plan.rows, LANES), f32),
@@ -333,7 +349,6 @@
         compiler_params=full,
         name="pack",
     )(records, halo_mass, forest_id, dest_block, dest_slot)
-    kept = (peers * plan.cap + plan.lab_tiles * LANES + 1024) * LANES * 4
     arrived, labels = pl.pallas_call(
         functools.partial(exchange_kernel, plan, n_ha),
         out_shape=(
@@ -341,15 +356,18 @@
             jax.ShapeDtypeStruct((plan.lab_tiles, LANES, LANES), i32),
         ),
         in_specs=[hbm],
-        out_specs=(vmem, vmem),
+        out_specs=(hbm, hbm),
         scratch_shapes=[
             pltpu.VMEM(send.shape, f32),
+            pltpu.VMEM((peers * plan.cap, LANES), f32),
+            pltpu.VMEM((plan.lab_tiles, LANES, LANES), i32),
             pltpu.SemaphoreType.DMA((peers,)),
             pltpu.SemaphoreType.DMA((peers,)),
             pltpu.SemaphoreType.DMA,
+            pltpu.SemaphoreType.DMA((peers + 1,)),
         ],
         compiler_params=pltpu.CompilerParams(
-            collective_id=0, has_side_effects=True, vmem_limit_bytes=67043328 - kept),
+            collective_id=0, has_side_effects=True, vmem_limit_bytes=67043328),
         name="exchange",
     )(send)
     blocks, block_mass, forest_mass, mean, second = pl.pallas_call(
@@ -361,16 +379,18 @@
             jax.ShapeDtypeStruct((fields, FOR_DEV), f32),
             jax.ShapeDtypeStruct((fields, FOR_DEV), f32),
         ),
-        in_specs=[vmem, vmem],
+        in_specs=[hbm, hbm],
         out_specs=(vmem,) * 5,
         scratch_shapes=[
+            pltpu.VMEM((peers * plan.cap, LANES), f32),
             pltpu.VMEM((plan.slots + 8, LANES), f32),
             pltpu.VMEM((10, FOR_DEV, 4 * LANES), jnp.bfloat16),
             pltpu.VMEM((10, 4 * LANES, 2 * LANES), jnp.bfloat16),
             pltpu.SMEM((plan.lab_tiles, LANES, LANES), i32),
             pltpu.SemaphoreType.DMA,
+            pltpu.SemaphoreType.DMA((peers,)),
         ],
-        compiler_params=big,
+        compiler_params=full,
         name="unpack",
     )(arrived, labels)
     return (

time: 64.5 us -> 68.4 us (1.060)
  Pallas kernels: 60.9 us -> 67.5 us
  local copies, waits for them, and re-layouts: 2.71 us -> 0 us
    pallas_call x1, Pallas kernels: 12.7 us -> 20.2 us  [on_device(): pl.pallas_call(functools.partial(unpack_kernel, plan), out_shape=(jax.Sha...]
    unnamed x4 -> x0, local copies, waits for them, and re-layouts: 2.71 us -> none
    pallas_call x1, Pallas kernels: 39.5 us -> 38.7 us  [on_device(): pl.pallas_call(functools.partial(exchange_kernel, plan, n_ha), out_shape=...]
where the time goes in v3:
time: 68.4 us; the launch traced here: 68.2 us
  Pallas kernels  67.5 us (99%)
    pallas_call x1, Pallas kernels, on_device(): pl.pallas_call(functools.partial(exchange_kernel, plan, n_ha), out_shape=...  38.7 us
    pallas_call x1, Pallas kernels, on_device(): pl.pallas_call(functools.partial(unpack_kernel, plan), out_shape=(jax.Sha...  20.2 us
    pallas_call x1, Pallas kernels, on_device(): pl.pallas_call(functools.partial(pack_kernel, plan), out_shape=jax.ShapeD...  8.69 us

profile of v3, /device:TPU:9, one launch (start us, length us, event | category | flops | bytes accessed | tf_op | source)
XLA Modules:
  0.0 68.2 jit_solution(1179131008617471871)
XLA Ops:
  0.6 8.7 %pack.1.send_ref = f32[8,376,128]{2,1,0:T(8,128)} custom-call(f32[64,4,1024]{2,1,0:T(4,128)} %rec_hbm.1, f32[4,1024]{1,0:T(4,128)} %mass_hbm.1, s32[4,1024]{1,0:T(4,128)} %forest_hbm.1, s32[4,1024]{1,0:T(4,128)} %block_hbm.1, s32[4,1024]{1,0:T(4,128)} %slot_hbm.1), custom_call_target="tpu_custom_call" | custom-call | tf_op jit(solution)/shard_map/pack/pallas_call | solution.py:327
  9.3 38.7 %exchange.1 = (f32[5632,128]{1,0:T(8,128)}, s32[2,128,128]{2,1,0:T(8,128)}) custom-call(f32[8,376,128]{2,1,0:T(8,128)} %pack.1.send_ref), custom_call_target="tpu_custom_call" | custom-call | tf_op jit(solution)/shard_map/exchange/pallas_call | solution.py:352
  48.0 20.2 %unpack.1 = (f32[2560,128]{1,0:T(8,128)}, f32[40,128]{1,0:T(8,128)}, f32[1,128]{1,0:T(1,128)}, f32[64,128]{1,0:T(8,128)}, f32[64,128]{1,0:T(8,128)}) custom-call(f32[5632,128]{1,0:T(8,128)} %get-tuple-element.12.arrived_hbm, s32[2,128,128]{2,1,0:T(8,128)} %get-tuple-element.13.labels), custom_call_target="tpu_custom_call" | custom-call | tf_op jit(solution)/shard_map/unpack/pallas_call | solution.py:373

commit v4 on v3

--- a/solution.py
+++ b/solution.py
@@ -260,18 +260,26 @@
     lax.fori_loop(0, plan.slots // 64, clear, 0)
     copy.wait()
 
-    def scatter(peer, carry):
-        tile = lax.div(peer, jnp.int32(plan.per_tile))
-        offset = lax.rem(peer, jnp.int32(plan.per_tile)) * plan.lab_rows
-        start = peer * plan.cap
+    for peer in range(peers):
+        tile, offset = peer // plan.per_tile, peer % plan.per_tile * plan.lab_rows
+        together = 3
+        trips = plan.cap // (together * plan.lab_rows)
+
+        def scatter(trip, carry, count=together * plan.lab_rows, peer=peer, tile=tile,
+                    offset=offset):
+            first = trip * together
+            for rank in range(count):
+                group, row = rank // plan.lab_rows, rank % plan.lab_rows
+                to = labels_s[tile, (first + group) * LABELS + 1, offset + row]
+                placed[pl.ds(to, 1), :] = arrived[
+                    pl.ds(peer * plan.cap + first * plan.lab_rows + rank, 1), :]
+            return carry
+
         take(peer).wait()
-        for rank in range(plan.cap):
-            group, row = rank // plan.lab_rows, rank % plan.lab_rows
-            to = labels_s[tile, group * LABELS + 1, offset + row]
-            placed[pl.ds(to, 1), :] = arrived[pl.ds(start + rank, 1), :]
-        return carry
-
-    lax.fori_loop(0, peers, scatter, 0)
+        lax.fori_loop(0, trips, scatter, 0)
+        rest = plan.cap - trips * together * plan.lab_rows
+        if rest:
+            scatter(trips, 0, count=rest)
 
     total = jnp.zeros((1, 1), jnp.float32)
     for peer in range(peers):

time: 68.4 us -> 61 us (0.89)
  Pallas kernels: 67.5 us -> 60.1 us
    pallas_call x1, Pallas kernels: 20.2 us -> 12.7 us  [on_device(): pl.pallas_call(functools.partial(unpack_kernel, plan), out_shape=(jax.Sha...]
where the time goes in v4:
time: 61 us; the launch traced here: 60.7 us
  Pallas kernels  60.1 us (99%)
  between operations  0.65 us (1%)
    pallas_call x1, Pallas kernels, on_device(): pl.pallas_call(functools.partial(exchange_kernel, plan, n_ha), out_shape=...  38.7 us
    pallas_call x1, Pallas kernels, on_device(): pl.pallas_call(functools.partial(unpack_kernel, plan), out_shape=(jax.Sha...  12.7 us
    pallas_call x1, Pallas kernels, on_device(): pl.pallas_call(functools.partial(pack_kernel, plan), out_shape=jax.ShapeD...  8.69 us

profile of v4, /device:TPU:9, one launch (start us, length us, event | category | flops | bytes accessed | tf_op | source)
XLA Modules:
  0.0 60.7 jit_solution(2731838674008062119)
XLA Ops:
  0.6 8.7 %pack.1.send_ref = f32[8,376,128]{2,1,0:T(8,128)} custom-call(f32[64,4,1024]{2,1,0:T(4,128)} %rec_hbm.1, f32[4,1024]{1,0:T(4,128)} %mass_hbm.1, s32[4,1024]{1,0:T(4,128)} %forest_hbm.1, s32[4,1024]{1,0:T(4,128)} %block_hbm.1, s32[4,1024]{1,0:T(4,128)} %slot_hbm.1), custom_call_target="tpu_custom_call" | custom-call | tf_op jit(solution)/shard_map/pack/pallas_call | solution.py:335
  9.3 38.7 %exchange.1 = (f32[5632,128]{1,0:T(8,128)}, s32[2,128,128]{2,1,0:T(8,128)}) custom-call(f32[8,376,128]{2,1,0:T(8,128)} %pack.1.send_ref), custom_call_target="tpu_custom_call" | custom-call | tf_op jit(solution)/shard_map/exchange/pallas_call | solution.py:360
  48.0 12.7 %unpack.1 = (f32[2560,128]{1,0:T(8,128)}, f32[40,128]{1,0:T(8,128)}, f32[1,128]{1,0:T(1,128)}, f32[64,128]{1,0:T(8,128)}, f32[64,128]{1,0:T(8,128)}) custom-call(f32[5632,128]{1,0:T(8,128)} %get-tuple-element.12.arrived_hbm, s32[2,128,128]{2,1,0:T(8,128)} %get-tuple-element.13.labels), custom_call_target="tpu_custom_call" | custom-call | tf_op jit(solution)/shard_map/unpack/pallas_call | solution.py:381
